TPU v7x, 32 devices: a whole 2x2x4 slice. The times are simulated.
32 devices in a mesh: dom: 8 (over z, core), group: 4 (over y, x).
Axes of the slice: x: 2, y: 2, z: 4, core: 2. Of those that a mesh axis runs over, the one named last changes fastest.
Arguments:
- start: bfloat16 [64, 32768], P(None, ('dom', 'group')), may hold values from -8.1 to 8.1
- tiles: int32 [32, 32, 128, 128], P(('dom', 'group')), may hold values from 0 to 15
- row_ptr: int32 [32, 9], P(('dom', 'group')), may hold values from 0 to 32, as said below
- col_part: int32 [32, 32], P(('dom', 'group')), may hold values from 0 to 7
- col_local: int32 [32, 32], P(('dom', 'group')), may hold values from 0 to 31, as said below
- halo_list: int32 [8, 8, 4], P('dom'), may hold values from 0 to 31
Outputs:
- vectors: bfloat16 [64, 32768], P(None, ('dom', 'group'))
- ritz: float32 [64, 64], replicated
Inputs may be any that keep to these rules, and one draw needn't show every extreme that they name: `row_ptr`: each row is strictly increasing from 0, so every block row has one or more slots; its last entry is at most 32 and equals 32 on some device row. `col_local`: below 32 where col_part names the row's own partition, below 4 otherwise.
All inputs are finite; a program needn't handle non-finite values.
Results may differ from a plain program's by a relative error of at most 0.012.
Values may be sent and summed in bfloat16 or wider, within the bound.
A program may use at most 64 MiB of HBM per device.

v0:
```python
import jax
import jax.numpy as jnp
from jax import lax
from jax.sharding import PartitionSpec as P

ITERS = 2


def shards(start, tiles, row_ptr, col_part, col_local, halo_list):
    own = lax.axis_index("dom")
    n_dom = lax.axis_size("dom")
    n_group = lax.axis_size("group")
    width = start.shape[0]
    rows_dev = start.shape[1]
    block = tiles.shape[2]
    slots = tiles.shape[1]
    block_rows = rows_dev // block
    halo = halo_list.shape[2]
    in_part = block_rows * n_group
    total_rows = rows_dev * n_dom * n_group
    pointers = row_ptr[0]
    counts = (pointers[1:] - pointers[:-1]).astype(jnp.float32)
    row_scale = 1.0 / (4.0 * jnp.sqrt(block * counts))
    slot_ids = jnp.arange(slots, dtype=jnp.int32)
    member = (
        (slot_ids[None, :] >= pointers[:-1, None]) & (slot_ids[None, :] < pointers[1:, None])
    ).astype(jnp.float32)
    centred = (tiles[0].astype(jnp.float32) - 7.5).astype(jnp.bfloat16)
    parts = col_part[0]
    places = col_local[0]
    pool_index = jnp.where(parts == own, places, in_part + parts * halo + places)
    targets = halo_list[0]

    def apply_graph(current):
        shaped = current.reshape(width, block_rows, block)
        part_blocks = lax.all_gather(shaped, "group", axis=1, tiled=True)
        outgoing = jnp.take(part_blocks, targets.reshape(-1), axis=1).reshape(
            width, n_dom, halo, block
        )
        incoming = lax.all_to_all(outgoing, "dom", split_axis=1, concat_axis=1, tiled=True)
        pool = jnp.concatenate([part_blocks, incoming.reshape(width, n_dom * halo, block)], axis=1)
        picked = jnp.take(pool, pool_index, axis=1)
        products = jnp.einsum("ksj,sij->ksi", picked, centred, preferred_element_type=jnp.float32)
        summed = jnp.einsum("rs,ksi->kri", member, products, precision=lax.Precision.HIGHEST)
        return (summed * row_scale[None, :, None]).reshape(width, rows_dev)

    current = start
    for step in range(ITERS):
        image = apply_graph(current)
        rounded = image.astype(jnp.bfloat16)
        local_gram = jnp.einsum("kn,ln->kl", rounded, rounded, preferred_element_type=jnp.float32)
        gram = lax.psum(local_gram, ("dom", "group")) / total_rows
        lower = jnp.linalg.cholesky(gram)
        current = lax.linalg.triangular_solve(
            lower, rounded.astype(jnp.float32), left_side=True, lower=True
        ).astype(jnp.bfloat16)
    final = apply_graph(current)
    local_ritz = jnp.einsum(
        "kn,ln->kl", current.astype(jnp.float32), final, precision=lax.Precision.HIGHEST
    )
    ritz = lax.psum(local_ritz, ("dom", "group")) / total_rows
    return (current, ritz)


def solution(mesh):
    return jax.shard_map(
        shards,
        mesh=mesh,
        in_specs=(
            P(None, ("dom", "group")),
            P(("dom", "group"), None, None, None),
            P(("dom", "group"), None),
            P(("dom", "group"), None),
            P(("dom", "group"), None),
            P("dom", None, None),
        ),
        out_specs=(P(None, ("dom", "group")), P()),
        check_vma=False,
    )
```

profile of v0, /device:TPU:0, one launch (start us, length us, event | category | flops | bytes accessed | tf_op | source)
XLA Modules:
  0.0 251.3 jit_solution(2166994840800570479)
XLA Ops:
  0.7 0.8 copy.50
  1.5 0.1 reshape_squeeze.2
  1.7 11.5 %all_gather.9 = bf16[64,32,128]{2,0,1:T(8,128)(2,1)S(1)} all-gather(bf16[64,8,128]{2,0,1:T(8,128)(2,1)S(1)} %copy_bitcast_fusion.2), channel_id=1, replica_groups=mesh['dom'=8,'group'=4] {'group'}, dimensions={1}, use_global_device_ids=true | all-gather | bytes 655360 | tf_op jit(solution)/shard_map/all_gather | solution.py:36
  13.2 0.6 gather_fusion
  13.8 0.9 broadcast_select_fusion.2
  14.7 5.0 %all-to-all-start = ((bf16[64,8,4,128]{3,0,2,1:T(8,128)(2,1)}), bf16[64,8,4,128]{3,0,2,1:T(8,128)(2,1)S(1)}, u32[]{:S(2)}, u32[]{:S(2)}) async-start(bf16[64,8,4,128]{3,0,2,1:T(8,128)(2,1)} %bitcast.5), calls=%async_computation | async-start | bytes 1048576 | tf_op jit(solution)/shard_map/all_to_all | solution.py:40
  19.8 0.1 multiply_divide_fusion
  19.9 0.1 slice_bitcast_fusion.1
  20.0 15.1 %all-to-all-done = bf16[64,8,4,128]{3,0,2,1:T(8,128)(2,1)S(1)} async-done(((bf16[64,8,4,128]{3,0,2,1:T(8,128)(2,1)}), bf16[64,8,4,128]{3,0,2,1:T(8,128)(2,1)S(1)}, u32[]{:S(2)}, u32[]{:S(2)}) %all-to-all-start) | async-done | bytes 524320 | tf_op jit(solution)/shard_map/all_to_all | solution.py:40
  35.1 1.1 pad_maximum_fusion
  36.2 1.9 gather_fusion.1
  38.1 0.8 convolution_bitcast_fusion.2
  38.9 1.1 fusion.3
  40.0 0.2 convolution_bitcast_fusion.4
  40.1 37.0 %psum.21 = f32[64,64]{0,1:T(8,128)S(1)} all-reduce(f32[64,64]{0,1:T(8,128)S(1)} %convolution_bitcast_fusion.4), channel_id=1, replica_groups=mesh['dom'=8,'group'=4] {'dom','group'}, use_global_device_ids=true, to_apply=%region_0.3 | all-reduce | flops 4096 | bytes 32768 | tf_op jit(solution)/shard_map/psum | solution.py:52
  77.2 0.1 copy.55
  77.3 5.8 %cholesky.44 = f32[64,64]{1,0:T(8,128)S(1)} custom-call(f32[64,64]{1,0:T(8,128)S(1)} %fusion.35), custom_call_target="Cholesky" | custom-call | tf_op jit(solution)/shard_map/jit(cholesky)/cholesky | solution.py:53
  83.1 0.6 compare_reduce_fusion.1
  83.8 0.7 fusion.30
  84.4 4.9 %custom-call.6 = f32[1,64,64]{1,2,0:T(8,128)S(1)} custom-call(f32[1,64,64]{2,1,0:T(8,128)S(1)} %fusion.30), custom_call_target="InvertDiagBlocksLowerTriangular" | custom-call | tf_op jit(solution)/shard_map/triangular_solve/custom-call.0 | solution.py:54
  89.4 0.4 fusion.4
  89.8 11.5 %all_gather.10 = bf16[64,32,128]{2,0,1:T(8,128)(2,1)S(1)} all-gather(bf16[64,8,128]{2,0,1:T(8,128)(2,1)S(1)} %bitcast.125), channel_id=1, replica_groups=mesh['dom'=8,'group'=4] {'group'}, dimensions={1}, use_global_device_ids=true | all-gather | bytes 655360 | tf_op jit(solution)/shard_map/all_gather | solution.py:36
  101.3 0.6 gather_fusion.2
  102.0 0.1 broadcast_select_fusion.1
  102.1 19.3 %all_to_all.15 = bf16[64,8,4,128]{3,0,2,1:T(8,128)(2,1)S(1)} all-to-all(bf16[64,8,4,128]{3,0,2,1:T(8,128)(2,1)S(1)} %bitcast.118), channel_id=1, replica_groups=mesh['dom'=8,'group'=4] {'dom'}, dimensions={1} | all-to-all | bytes 1048576 | tf_op jit(solution)/shard_map/all_to_all | solution.py:40
  121.4 1.1 pad_maximum_fusion.1
  122.5 1.9 gather_fusion.3
  124.4 0.8 convolution_bitcast_fusion.1
  125.2 1.1 fusion.2
  126.3 0.2 convolution_bitcast_fusion.3
  126.5 37.6 %psum.22 = f32[64,64]{0,1:T(8,128)S(1)} all-reduce(f32[64,64]{0,1:T(8,128)S(1)} %convolution_bitcast_fusion.3), channel_id=1, replica_groups=mesh['dom'=8,'group'=4] {'dom','group'}, use_global_device_ids=true, to_apply=%region_3.0 | all-reduce | flops 4096 | bytes 32768 | tf_op jit(solution)/shard_map/psum | solution.py:52
  164.1 0.1 copy.61
  164.2 5.8 %cholesky.55 = f32[64,64]{1,0:T(8,128)S(1)} custom-call(f32[64,64]{1,0:T(8,128)S(1)} %fusion.33), custom_call_target="Cholesky" | custom-call | tf_op jit(solution)/shard_map/jit(cholesky)/cholesky | solution.py:53
  170.0 0.6 compare_reduce_fusion
  170.7 0.7 fusion.31
  171.4 4.9 %custom-call.7 = f32[1,64,64]{1,2,0:T(8,128)S(1)} custom-call(f32[1,64,64]{2,1,0:T(8,128)S(1)} %fusion.31), custom_call_target="InvertDiagBlocksLowerTriangular" | custom-call | tf_op jit(solution)/shard_map/triangular_solve/custom-call.0 | solution.py:54
  176.3 0.4 convolution_convert_fusion
  176.8 11.5 %all_gather.11 = bf16[64,32,128]{2,0,1:T(8,128)(2,1)S(1)} all-gather(bf16[64,8,128]{2,0,1:T(8,128)(2,1)S(1)} %copy_bitcast_fusion), channel_id=1, replica_groups=mesh['dom'=8,'group'=4] {'group'}, dimensions={1}, use_global_device_ids=true | all-gather | bytes 655360 | tf_op jit(solution)/shard_map/all_gather | solution.py:36
  188.2 0.6 gather_fusion.4
  188.9 0.1 broadcast_select_fusion
  189.0 18.8 %all_to_all.16 = bf16[64,8,4,128]{3,0,2,1:T(8,128)(2,1)S(1)} all-to-all(bf16[64,8,4,128]{3,0,2,1:T(8,128)(2,1)S(1)} %bitcast.117), channel_id=1, replica_groups=mesh['dom'=8,'group'=4] {'dom'}, dimensions={1} | all-to-all | bytes 1048576 | tf_op jit(solution)/shard_map/all_to_all | solution.py:40
  207.8 1.1 pad_maximum_fusion.2
  208.9 1.9 gather_fusion.5
  210.8 0.8 convolution_bitcast_fusion
  211.6 1.1 convolution_multiply_fusion
  212.7 0.3 fusion.18
  213.0 37.6 %psum.23 = f32[64,64]{0,1:T(8,128)S(1)} all-reduce(f32[64,64]{0,1:T(8,128)S(1)} %fusion.18), channel_id=1, replica_groups=mesh['dom'=8,'group'=4] {'dom','group'}, use_global_device_ids=true, to_apply=%region_4.0 | all-reduce | flops 4096 | bytes 32768 | tf_op jit(solution)/shard_map/psum | solution.py:61
  250.6 0.7 copy.65
  (29 shorter events, 0.3 us)
Async XLA Ops:
  0.6 1.0 copy-start
  0.6 19.1 %copy-start.5 = (s32[1,32]{1,0:T(1,128)S(1)}, s32[1,32]{1,0:T(1,128)}, u32[]{:S(2)}) copy-start(s32[1,32]{1,0:T(1,128)} %param.17) | copy-start | bytes 388
  0.7 19.1 %copy-start.4 = (s32[1,32]{1,0:T(1,128)S(1)}, s32[1,32]{1,0:T(1,128)}, u32[]{:S(2)}) copy-start(s32[1,32]{1,0:T(1,128)} %param.16) | copy-start | bytes 388
  0.7 19.1 %copy-start.3 = (s32[1,9]{1,0:T(1,128)S(1)}, s32[1,9]{1,0:T(1,128)}, u32[]{:S(2)}) copy-start(s32[1,9]{1,0:T(1,128)} %param.15) | copy-start | bytes 112
  14.7 23.3 %copy-start.1 = (s32[1,32,128,128]{3,2,1,0:T(8,128)S(1)}, s32[1,32,128,128]{3,2,1,0:T(8,128)}, u32[]{:S(2)}) copy-start(s32[1,32,128,128]{3,2,1,0:T(8,128)} %param.14) | copy-start | bytes 6291460
  14.7 20.3 %all-to-all-start = ((bf16[64,8,4,128]{3,0,2,1:T(8,128)(2,1)}), bf16[64,8,4,128]{3,0,2,1:T(8,128)(2,1)S(1)}, u32[]{:S(2)}, u32[]{:S(2)}) async-start(bf16[64,8,4,128]{3,0,2,1:T(8,128)(2,1)} %bitcast.5), calls=%async_computation | async-start | bytes 1048576 | tf_op jit(solution)/shard_map/all_to_all | solution.py:40
  176.7 36.0 %copy-start.2 = (bf16[64,1024]{1,0:T(8,128)(2,1)}, bf16[64,1024]{1,0:T(8,128)(2,1)S(1)}, u32[]{:S(2)}) copy-start(bf16[64,1024]{1,0:T(8,128)(2,1)S(1)} %convolution_convert_fusion) | copy-start | bytes 393220
where the time goes:
time: 252 us; the launch traced here: 251 us
  blocking collectives  185 us (73%)
  other arithmetic  28.7 us (11%)
  waiting for transfers between devices  15.1 us (6%)
  local copies, waits for them, and re-layouts  9.49 us (4%)
  matrix products  7.18 us (3%)
  starting transfers between devices  5.01 us (2%)
    psum x2, blocking collectives, shards(): gram = lax.psum(local_gram, ('dom', 'group')) / total_rows  74.5 us
    all_to_all x2, blocking collectives, apply_graph(): lax.all_to_all(outgoing, 'dom', split_axis=1, concat_axis=1, tiled=True)  38.2 us
    psum x1, blocking collectives, shards(): ritz = lax.psum(local_ritz, ('dom', 'group')) / total_rows  37.6 us
    all_gather x3, blocking collectives, apply_graph(): part_blocks = lax.all_gather(shaped, 'group', axis=1, tiled=True)  34.5 us
    all_to_all x1, waiting for transfers between devices, apply_graph(): lax.all_to_all(outgoing, 'dom', split_axis=1, concat_axis=1, tiled=True)  15.1 us
    another operation x6, other arithmetic, shards(): lower = jnp.linalg.cholesky(gram)  13 us
    another operation x4, other arithmetic, shards(): lax.linalg.triangular_solve(lower, rounded.astype(jnp.float32), left_side...  11.1 us
    gather x3, local copies, waits for them, and re-layouts, apply_graph(): picked = jnp.take(pool, pool_index, axis=1)  5.61 us
  transfers between devices with their start and end apart: 1, of which 1 were waited for; matrix products, arithmetic and copies ran while one was open for 0% of the time, Pallas kernels for 0%

commit v1 on v0

v1 whole, which is shorter than its diff:
```python
import functools

import jax
import jax.numpy as jnp
from jax import lax
from jax.experimental import pallas as pl
from jax.experimental.pallas import tpu as pltpu
from jax.sharding import PartitionSpec as P

ITERS = 2
MESH = pl.DeviceIdType.MESH
HIGH = lax.Precision.HIGHEST
CHUNK = 8


def dot(a, b, dims=((1,), (0,)), precision=None):
    return lax.dot_general(a, b, (dims, ((), ())), precision=precision, preferred_element_type=jnp.float32)


def inverse_factor(gram):
    k = gram.shape[0]
    rows = lax.broadcasted_iota(jnp.int32, (k, k), 0)
    cols = lax.broadcasted_iota(jnp.int32, (k, k), 1)
    work = jnp.concatenate([gram, jnp.where(rows == cols, 1.0, 0.0).astype(jnp.float32)], axis=1)
    row_ids = lax.broadcasted_iota(jnp.int32, (k, 1), 0)
    pivots = jnp.zeros((k, 1), jnp.float32)
    for i in range(k):
        column = work[:, i : i + 1]
        pivot = work[i : i + 1, i : i + 1]
        pivots = jnp.where(row_ids == i, pivot, pivots)
        factor = jnp.where(row_ids > i, column / pivot, 0.0)
        work = work - factor * work[i : i + 1, :]
    return work[:, k:] * (1.0 / jnp.sqrt(pivots))


def kernel(n_dom, n_group, halo, total_rows, *refs):
    start_ref, tiles_ref, ptr_ref, cpart_ref, cloc_ref, halo_ref, vec_ref, ritz_ref = refs[:8]
    refs = refs[8:]
    n_apply = ITERS + 1
    parts, refs = refs[:n_apply], refs[n_apply:]
    halos, refs = refs[:n_apply], refs[n_apply:]
    stages, refs = refs[:n_apply], refs[n_apply:]
    raw, tb, prod, rounded_ref = refs[:4]
    refs = refs[4:]
    g_src, refs = refs[:n_apply], refs[n_apply:]
    g_one, refs = refs[:n_apply], refs[n_apply:]
    g_two, refs = refs[:n_apply], refs[n_apply:]
    g_all, refs = refs[:n_apply], refs[n_apply:]
    tile_sem, s1, r1, s2, r2, s3, r3, sa, ra, sb, rb, sc, rc = refs

    own = lax.axis_index("dom")
    me = lax.axis_index("group")
    slots, block = tb.shape[0], tb.shape[1]
    width = start_ref.shape[0]
    block_rows = start_ref.shape[1] // block
    per = max(1, halo // n_group)
    senders = halo // per
    gram_rows = width // n_group
    doms = []
    for step in range(1, n_dom // 2 + 1):
        doms.append(step)
        if n_dom - step != step:
            doms.append(n_dom - step)

    def up(offset):
        return lax.rem(own + offset, n_dom)

    def beside(offset):
        return lax.rem(me + offset, n_group)

    def as_sender(index, body):
        if senders == n_group:
            body()
        else:
            pl.when(index < senders)(body)

    def remote(src, dst, send_sem, recv_sem, device):
        return pltpu.make_async_remote_copy(
            src_ref=src, dst_ref=dst, send_sem=send_sem, recv_sem=recv_sem, device_id=device, device_id_type=MESH
        )

    barrier = pltpu.get_barrier_semaphore()
    for offset in range(1, n_group):
        pl.semaphore_signal(barrier, inc=1, device_id=(own, beside(offset)), device_id_type=MESH)
    for offset in range(1, n_dom):
        pl.semaphore_signal(barrier, inc=1, device_id=(up(offset), me), device_id_type=MESH)

    n_chunks = slots // CHUNK
    loads = [
        pltpu.make_async_copy(
            tiles_ref.at[0, pl.ds(c * CHUNK, CHUNK)], raw.at[pl.ds(c * CHUNK, CHUNK)], tile_sem.at[c]
        )
        for c in range(n_chunks)
    ]
    for load in loads:
        load.start()

    def put_own(a, values):
        for b in range(block_rows):
            parts[a][me * block_rows + b] = values[:, b * block : (b + 1) * block]

    def first_copies(a):
        mine = pl.ds(me * block_rows, block_rows)
        return [
            remote(parts[a].at[mine], parts[a].at[mine], s1.at[a, o], r1.at[a, o], (own, beside(o)))
            for o in range(1, n_group)
        ]

    def second_copies(a):
        place = pl.ds(own * halo + me * per, per)
        return [
            remote(stages[a].at[o], halos[a].at[place], s2.at[a, o], r2.at[a, o], (up(o), me)) for o in doms
        ]

    def third_copies(a, o):
        place = pl.ds(up(n_dom - o) * halo + me * per, per)
        return [
            remote(halos[a].at[place], halos[a].at[place], s3.at[a, o, j], r3.at[a, o, j], (own, beside(j)))
            for j in range(1, n_group)
        ]

    def exchange_second(a):
        for copy in first_copies(a):
            copy.wait_recv()

        def body():
            for o in doms:
                for h in range(per):
                    stages[a][o, h] = parts[a][halo_ref[0, up(o), me * per + h]]
            for copy in second_copies(a):
                copy.start()

        as_sender(me, body)

    def exchange_third(a):
        def body():
            for o, copy in zip(doms, second_copies(a)):
                copy.wait_recv()
                for spread in third_copies(a, o):
                    spread.start()

        as_sender(me, body)

    def exchange_end(a):
        for o in doms:
            for j, copy in zip(range(1, n_group), third_copies(a, o)):
                as_sender(beside(n_group - j), copy.wait_recv)

    def exchange_sends(a):
        for copy in first_copies(a):
            copy.wait_send()

        def body():
            for o, copy in zip(doms, second_copies(a)):
                copy.wait_send()
                for spread in third_copies(a, o):
                    spread.wait_send()

        as_sender(me, body)

    def apply_graph(a):
        prod[0] = jnp.zeros((width, block), jnp.float32)

        def body(c, total):
            for i in range(CHUNK):
                s = c * CHUNK + i
                here = cpart_ref[0, s] == own
                near = parts[a][jnp.where(here, cloc_ref[0, s], 0)]
                far = halos[a][jnp.where(here, 0, cpart_ref[0, s] * halo + cloc_ref[0, s])]
                picked = jnp.where(here, near, far)
                total = total + dot(picked, tb[s], ((1,), (1,)))
                prod[s + 1] = total
            return total

        lax.fori_loop(0, n_chunks, body, jnp.zeros((width, block), jnp.float32))
        out = []
        for r in range(block_rows):
            low, high = ptr_ref[0, r], ptr_ref[0, r + 1]
            count = jnp.full((1, block), high - low, jnp.int32).astype(jnp.float32)
            scale = 1.0 / (4.0 * jnp.sqrt(block * count))
            out.append((prod[high] - prod[low]) * scale)
        return jnp.concatenate(out, axis=1)

    def sum_one(t, value):
        padded = jnp.concatenate([value, jnp.zeros((width, block - width), jnp.float32)], axis=1)
        g_src[t][...] = padded.reshape(n_group, gram_rows, block)
        g_one[t][me] = g_src[t][me]
        copies = [
            remote(g_src[t].at[beside(o)], g_one[t].at[me], sa.at[t, o], ra.at[t, o], (own, beside(o)))
            for o in range(1, n_group)
        ]
        for copy in copies:
            copy.start()
        return copies

    def sum_two(t, copies):
        for copy in copies:
            copy.wait_recv()
        total = g_one[t][0]
        for j in range(1, n_group):
            total = total + g_one[t][j]
        g_two[t][own] = total
        more = [
            remote(g_two[t].at[own], g_two[t].at[own], sb.at[t, o], rb.at[t, o], (up(o), me)) for o in doms
        ]
        for copy in more:
            copy.start()
        return more

    def sum_three(t, copies):
        for copy in copies:
            copy.wait_recv()
        total = g_two[t][0]
        for j in range(1, n_dom):
            total = total + g_two[t][j]
        g_all[t][me] = total * (1.0 / total_rows)
        more = [
            remote(g_all[t].at[me], g_all[t].at[me], sc.at[t, o], rc.at[t, o], (own, beside(o)))
            for o in range(1, n_group)
        ]
        for copy in more:
            copy.start()
        return more

    def sum_end(t, copies):
        for copy in copies:
            copy.wait_recv()
        return g_all[t][...].reshape(width, block)[:, :width]

    put_own(0, start_ref[...])
    pl.semaphore_wait(barrier, n_group - 1 + n_dom - 1)
    for copy in first_copies(0):
        copy.start()

    for c, load in enumerate(loads):
        load.wait()

        def convert(i, carry):
            s = c * CHUNK + i
            tb[s] = (raw[s].astype(jnp.float32) - 7.5).astype(jnp.bfloat16)
            return carry

        lax.fori_loop(0, CHUNK, convert, 0)

    exchange_second(0)
    exchange_third(0)
    exchange_end(0)

    pending = []
    inverse = None
    for t in range(ITERS):
        image = apply_graph(t)
        if t > 0:
            image = dot(inverse, image, precision=HIGH)
        rounded = image.astype(jnp.bfloat16)
        put_own(t + 1, rounded)
        for copy in first_copies(t + 1):
            copy.start()
        rounded_ref[...] = rounded
        one = sum_one(t, dot(rounded, rounded, ((1,), (1,))))
        exchange_second(t + 1)
        two = sum_two(t, one)
        exchange_third(t + 1)
        three = sum_three(t, two)
        inverse = inverse_factor(sum_end(t, three))
        pending += one + two + three
        if t == ITERS - 1:
            vectors = dot(inverse, rounded_ref[...].astype(jnp.float32), precision=HIGH).astype(jnp.bfloat16)
            vec_ref[...] = vectors
        exchange_end(t + 1)

    final = dot(inverse, apply_graph(ITERS), precision=HIGH)
    local = dot(vec_ref[...].astype(jnp.float32), final, ((1,), (1,)), precision=HIGH)
    one = sum_one(ITERS, local)
    two = sum_two(ITERS, one)
    three = sum_three(ITERS, two)
    ritz_ref[...] = sum_end(ITERS, three)
    pending += one + two + three
    for copy in pending:
        copy.wait_send()
    for a in range(n_apply):
        exchange_sends(a)


def solution(mesh):
    n_dom, n_group = mesh.shape["dom"], mesh.shape["group"]
    n_apply = ITERS + 1

    def step(start, tiles, row_ptr, col_part, col_local, halo_list):
        width, rows_dev = start.shape
        slots, block = tiles.shape[1], tiles.shape[2]
        halo = halo_list.shape[2]
        in_part = rows_dev // block * n_group
        per = max(1, halo // n_group)
        gram_rows = width // n_group
        vmem = pl.BlockSpec(memory_space=pltpu.VMEM)
        smem = pl.BlockSpec(memory_space=pltpu.SMEM)
        dma = pltpu.SemaphoreType.DMA
        return pl.pallas_call(
            functools.partial(kernel, n_dom, n_group, halo, rows_dev * n_dom * n_group),
            out_shape=(
                jax.ShapeDtypeStruct((width, rows_dev), jnp.bfloat16),
                jax.ShapeDtypeStruct((width, width), jnp.float32),
            ),
            in_specs=[vmem, pl.BlockSpec(memory_space=pl.ANY), smem, smem, smem, smem],
            out_specs=(vmem, vmem),
            scratch_shapes=(
                [pltpu.VMEM((in_part, width, block), jnp.bfloat16)] * n_apply
                + [pltpu.VMEM((n_dom * halo, width, block), jnp.bfloat16)] * n_apply
                + [pltpu.VMEM((n_dom, per, width, block), jnp.bfloat16)] * n_apply
                + [
                    pltpu.VMEM((slots, block, block), jnp.int32),
                    pltpu.VMEM((slots, block, block), jnp.bfloat16),
                    pltpu.VMEM((slots + 1, width, block), jnp.float32),
                    pltpu.VMEM((width, rows_dev), jnp.bfloat16),
                ]
                + [pltpu.VMEM((n_group, gram_rows, block), jnp.float32)] * n_apply
                + [pltpu.VMEM((n_group, gram_rows, block), jnp.float32)] * n_apply
                + [pltpu.VMEM((n_dom, gram_rows, block), jnp.float32)] * n_apply
                + [pltpu.VMEM((n_group, gram_rows, block), jnp.float32)] * n_apply
                + [dma((slots // CHUNK,))]
                + [dma((n_apply, n_group))] * 2
                + [dma((n_apply, n_dom))] * 2
                + [dma((n_apply, n_dom, n_group))] * 2
                + [dma((n_apply, n_group))] * 2
                + [dma((n_apply, n_dom))] * 2
                + [dma((n_apply, n_group))] * 2
            ),
            compiler_params=pltpu.CompilerParams(
                collective_id=0, has_side_effects=True, vmem_limit_bytes=48 * 1024 * 1024
            ),
        )(start, tiles, row_ptr, col_part, col_local, halo_list)

    return jax.shard_map(
        step,
        mesh=mesh,
        in_specs=(
            P(None, ("dom", "group")),
            P(("dom", "group"), None, None, None),
            P(("dom", "group"), None),
            P(("dom", "group"), None),
            P(("dom", "group"), None),
            P("dom", None, None),
        ),
        out_specs=(P(None, ("dom", "group")), P()),
        check_vma=False,
    )
```

time: 252 us -> 94.7 us (0.38)
  blocking collectives: 185 us -> 0 us
  Pallas kernels: 0 us -> 87.4 us
  other arithmetic: 28.7 us -> 0 us
  waiting for transfers between devices: 15.1 us -> 0 us
  matrix products: 7.18 us -> 0 us
  starting transfers between devices: 5.01 us -> 0 us
  local copies, waits for them, and re-layouts: 9.49 us -> 6.49 us
    psum x3 -> x0, blocking collectives: 112 us -> none  [the longest x2 74.5 us: shards(): gram = lax.psum(local_gram, ('dom', 'group')) / total_rows]
    pallas_call x0 -> x1, Pallas kernels: none -> 87.4 us  [step(): pl.pallas_call(functools.partial(kernel, n_dom, n_group, halo, rows_dev *...]
    all_to_all x2 -> x0, blocking collectives: 38.2 us -> none  [apply_graph(): lax.all_to_all(outgoing, 'dom', split_axis=1, concat_axis=1, tiled=True)]
    all_gather x3 -> x0, blocking collectives: 34.5 us -> none  [apply_graph(): part_blocks = lax.all_gather(shaped, 'group', axis=1, tiled=True)]
    another operation x10 -> x0, other arithmetic: 24.1 us -> none  [the longest x6 13 us: shards(): lower = jnp.linalg.cholesky(gram)]
    all_to_all x1 -> x0, waiting for transfers between devices: 15.1 us -> none  [apply_graph(): lax.all_to_all(outgoing, 'dom', split_axis=1, concat_axis=1, tiled=True)]
    gather x6 -> x0, local copies, waits for them, and re-layouts: 7.56 us -> none  [the longest x3 5.61 us: apply_graph(): picked = jnp.take(pool, pool_index, axis=1)]
    dot_general x9 -> x0, matrix products: 6.33 us -> none  [the longest x3 3.19 us: apply_graph(): jnp.einsum('rs,ksi->kri', member, products, precision=lax.Precision.HIGHEST)]
  transfers between devices with their start and end apart: 1 -> 0, of which waited for: 1 -> 0; matrix products, arithmetic and copies ran while one was open for 0% -> 0% of each run, Pallas kernels for 0% -> 0%
where the time goes in v1:
time: 94.7 us; the launch traced here: 94.5 us
  Pallas kernels  87.4 us (92%)
  local copies, waits for them, and re-layouts  6.49 us (7%)
    pallas_call x1, Pallas kernels, step(): pl.pallas_call(functools.partial(kernel, n_dom, n_group, halo, rows_dev *...  87.4 us
    unnamed x13, local copies, waits for them, and re-layouts  6.49 us

profile of v1, /device:TPU:0, one launch (start us, length us, event | category | flops | bytes accessed | tf_op | source)
XLA Modules:
  0.0 94.5 jit_solution(8608040929728027599)
XLA Ops:
  0.6 0.8 copy.8.refs_5_
  1.4 0.0 copy-start
  1.4 1.6 %copy-done = s32[1,32,128,128]{3,2,1,0:T(8,128)S(1)} copy-done((s32[1,32,128,128]{3,2,1,0:T(8,128)S(1)}, s32[1,32,128,128]{3,2,1,0:T(8,128)}, u32[]{:S(2)}) %copy-start) | copy-done | bytes 2097176
  3.0 0.0 copy-start.1
  3.0 0.9 copy-done.1
  3.9 0.0 copy-start.2
  3.9 0.7 copy-done.2
  4.5 0.0 copy-start.3
  4.5 0.7 copy-done.3
  5.2 0.0 copy-start.4
  5.2 0.7 copy-done.4
  5.8 87.4 %shard_map.77 = (bf16[64,1024]{1,0:T(8,128)(2,1)S(1)}, f32[64,64]{1,0:T(8,128)S(1)}) custom-call(bf16[64,1024]{1,0:T(8,128)(2,1)S(1)} %copy-done.1, s32[1,32,128,128]{3,2,1,0:T(8,128)S(1)} %copy-done, s32[1,9]{1,0:T(1,128)S(1)} %copy-done.2, s32[1,32]{1,0:T(1,128)S(1)} %copy-done.3, s32[1,32]{1,0:T(1,128)S(1)} %copy-done.4, s32[1,8,4]{2,1,0:T(8,128)S(1)} %copy.8.refs_5_), custom_call_target="tpu_custom_call" | custom-call | tf_op jit(solution)/shard_map/pallas_call | solution.py:299
  93.2 0.7 copy.11
  93.9 0.6 copy.12
Async XLA Ops:
  1.4 1.6 %copy-start = (s32[1,32,128,128]{3,2,1,0:T(8,128)S(1)}, s32[1,32,128,128]{3,2,1,0:T(8,128)}, u32[]{:S(2)}) copy-start(s32[1,32,128,128]{3,2,1,0:T(8,128)} %refs_1_.1) | copy-start | bytes 6291460
  3.0 0.9 copy-start.1
  3.9 0.7 copy-start.2
  4.5 0.7 copy-start.3
  5.2 0.7 copy-start.4

commit v2 on v1

--- a/solution.py
+++ b/solution.py
@@ -11,31 +11,49 @@
 MESH = pl.DeviceIdType.MESH
 HIGH = lax.Precision.HIGHEST
 CHUNK = 8
+PANEL = 4
 
 
 def dot(a, b, dims=((1,), (0,)), precision=None):
     return lax.dot_general(a, b, (dims, ((), ())), precision=precision, preferred_element_type=jnp.float32)
 
 
-def inverse_factor(gram):
+def factor_start(gram):
     k = gram.shape[0]
     rows = lax.broadcasted_iota(jnp.int32, (k, k), 0)
     cols = lax.broadcasted_iota(jnp.int32, (k, k), 1)
     work = jnp.concatenate([gram, jnp.where(rows == cols, 1.0, 0.0).astype(jnp.float32)], axis=1)
-    row_ids = lax.broadcasted_iota(jnp.int32, (k, 1), 0)
-    pivots = jnp.zeros((k, 1), jnp.float32)
-    for i in range(k):
-        column = work[:, i : i + 1]
-        pivot = work[i : i + 1, i : i + 1]
-        pivots = jnp.where(row_ids == i, pivot, pivots)
-        factor = jnp.where(row_ids > i, column / pivot, 0.0)
-        work = work - factor * work[i : i + 1, :]
-    return work[:, k:] * (1.0 / jnp.sqrt(pivots))
+    return work, jnp.ones(work.shape, jnp.float32)
+
+
+def factor_steps(state, first, last):
+    work, pivots = state
+    row_ids = lax.broadcasted_iota(jnp.int32, work.shape, 0)
+    for i in range(first, last, PANEL):
+        cols = [jnp.broadcast_to(work[:, i + b : i + b + 1], work.shape) for b in range(PANEL)]
+        rows = [work[i + b : i + b + 1, :] for b in range(PANEL)]
+        for b in range(PANEL):
+            pivot = cols[b][i + b : i + b + 1, :]
+            inv = 1.0 / pivot
+            pivots = jnp.where(row_ids == i + b, pivot, pivots)
+            for c in range(b + 1, PANEL):
+                ratio = cols[c][i + b : i + b + 1, :] * inv
+                rows[c] = rows[c] - (cols[b][i + c : i + c + 1, :] * inv) * rows[b]
+                cols[c] = cols[c] - cols[b] * ratio
+            work = work - jnp.where(row_ids > i + b, cols[b], 0.0) * (rows[b] * inv)
+    return work, pivots
+
+
+def factor_end(state):
+    work, pivots = state
+    k = work.shape[0]
+    return work[:, k:] * (1.0 / jnp.sqrt(pivots[:, k:]))
 
 
 def kernel(n_dom, n_group, halo, total_rows, *refs):
-    start_ref, tiles_ref, ptr_ref, cpart_ref, cloc_ref, halo_ref, vec_ref, ritz_ref = refs[:8]
-    refs = refs[8:]
+    start_hbm, tiles_ref, ptr_hbm, cpart_hbm, cloc_hbm, halo_hbm, vec_ref, ritz_ref = refs[:8]
+    start_ref, ptr_ref, cpart_ref, cloc_ref, halo_ref, in_sem = refs[8:14]
+    refs = refs[14:]
     n_apply = ITERS + 1
     parts, refs = refs[:n_apply], refs[n_apply:]
     halos, refs = refs[:n_apply], refs[n_apply:]
@@ -79,6 +97,21 @@
             src_ref=src, dst_ref=dst, send_sem=send_sem, recv_sem=recv_sem, device_id=device, device_id_type=MESH
         )
 
+    smalls = [
+        pltpu.make_async_copy(src, dst, in_sem.at[i])
+        for i, (src, dst) in enumerate(
+            [
+                (start_hbm, start_ref),
+                (ptr_hbm, ptr_ref),
+                (cpart_hbm, cpart_ref),
+                (cloc_hbm, cloc_ref),
+                (halo_hbm, halo_ref),
+            ]
+        )
+    ]
+    for load in smalls:
+        load.start()
+
     barrier = pltpu.get_barrier_semaphore()
     for offset in range(1, n_group):
         pl.semaphore_signal(barrier, inc=1, device_id=(own, beside(offset)), device_id_type=MESH)
@@ -99,28 +132,61 @@
         for b in range(block_rows):
             parts[a][me * block_rows + b] = values[:, b * block : (b + 1) * block]
 
+    relayed = n_group == 4
+    half = block_rows // 2
+    across = me + 1 - 2 * lax.rem(me, 2)
+    along = beside(n_group // 2)
+
+    def half_copy(a, who, part, index, to):
+        place = pl.ds(who * block_rows + part * half, half)
+        return remote(parts[a].at[place], parts[a].at[place], s1.at[a, index], r1.at[a, index], (own, to))
+
     def first_copies(a):
+        if relayed:
+            return [
+                half_copy(a, me, 0, 0, across),
+                half_copy(a, me, 1, 1, along),
+                half_copy(a, me, 1, 2, across),
+                half_copy(a, me, 0, 3, along),
+            ]
         mine = pl.ds(me * block_rows, block_rows)
         return [
             remote(parts[a].at[mine], parts[a].at[mine], s1.at[a, o], r1.at[a, o], (own, beside(o)))
             for o in range(1, n_group)
         ]
 
+    def relay_copies(a):
+        return [half_copy(a, across, 0, 4, along), half_copy(a, along, 1, 5, across)]
+
+    def exchange_relay(a):
+        if relayed:
+            for copy, relay in zip(first_copies(a)[:2], relay_copies(a)):
+                copy.wait_recv()
+                relay.start()
+
     def second_copies(a):
         place = pl.ds(own * halo + me * per, per)
         return [
             remote(stages[a].at[o], halos[a].at[place], s2.at[a, o], r2.at[a, o], (up(o), me)) for o in doms
         ]
 
+    def third_copy(a, o, who, index, to):
+        place = pl.ds(up(n_dom - o) * halo + who * per, per)
+        return remote(halos[a].at[place], halos[a].at[place], s3.at[a, o, index], r3.at[a, o, index], (own, to))
+
     def third_copies(a, o):
-        place = pl.ds(up(n_dom - o) * halo + me * per, per)
-        return [
-            remote(halos[a].at[place], halos[a].at[place], s3.at[a, o, j], r3.at[a, o, j], (own, beside(j)))
-            for j in range(1, n_group)
-        ]
+        if relayed:
+            return [third_copy(a, o, me, 0, across), third_copy(a, o, me, 1, along)]
+        return [third_copy(a, o, me, j, beside(j)) for j in range(1, n_group)]
+
+    def third_relay(a, o):
+        if doms.index(o) % 2:
+            return third_copy(a, o, along, 2, across)
+        return third_copy(a, o, across, 2, along)
 
     def exchange_second(a):
-        for copy in first_copies(a):
+        rest = first_copies(a)[2:] + relay_copies(a) if relayed else first_copies(a)
+        for copy in rest:
             copy.wait_recv()
 
         def body():
@@ -142,12 +208,20 @@
         as_sender(me, body)
 
     def exchange_end(a):
+        if relayed:
+            for o in doms:
+                for copy in third_copies(a, o):
+                    copy.wait_recv()
+                third_relay(a, o).start()
+            for o in doms:
+                third_relay(a, o).wait_recv()
+            return
         for o in doms:
             for j, copy in zip(range(1, n_group), third_copies(a, o)):
                 as_sender(beside(n_group - j), copy.wait_recv)
 
     def exchange_sends(a):
-        for copy in first_copies(a):
+        for copy in first_copies(a) + (relay_copies(a) if relayed else []):
             copy.wait_send()
 
         def body():
@@ -155,6 +229,8 @@
                 copy.wait_send()
                 for spread in third_copies(a, o):
                     spread.wait_send()
+                if relayed:
+                    third_relay(a, o).wait_send()
 
         as_sender(me, body)
 
@@ -227,6 +303,8 @@
             copy.wait_recv()
         return g_all[t][...].reshape(width, block)[:, :width]
 
+    for load in smalls:
+        load.wait()
     put_own(0, start_ref[...])
     pl.semaphore_wait(barrier, n_group - 1 + n_dom - 1)
     for copy in first_copies(0):
@@ -234,6 +312,8 @@
 
     for c, load in enumerate(loads):
         load.wait()
+        if c == n_chunks // 2:
+            exchange_relay(0)
 
         def convert(i, carry):
             s = c * CHUNK + i
@@ -254,15 +334,18 @@
             image = dot(inverse, image, precision=HIGH)
         rounded = image.astype(jnp.bfloat16)
         put_own(t + 1, rounded)
+        rounded_ref[...] = rounded
+        one = sum_one(t, dot(rounded, rounded, ((1,), (1,))))
         for copy in first_copies(t + 1):
             copy.start()
-        rounded_ref[...] = rounded
-        one = sum_one(t, dot(rounded, rounded, ((1,), (1,))))
+        two = sum_two(t, one)
+        exchange_relay(t + 1)
+        three = sum_three(t, two)
         exchange_second(t + 1)
-        two = sum_two(t, one)
+        state = factor_start(sum_end(t, three))
+        state = factor_steps(state, 0, width // 2)
         exchange_third(t + 1)
-        three = sum_three(t, two)
-        inverse = inverse_factor(sum_end(t, three))
+        inverse = factor_end(factor_steps(state, width // 2, width))
         pending += one + two + three
         if t == ITERS - 1:
             vectors = dot(inverse, rounded_ref[...].astype(jnp.float32), precision=HIGH).astype(jnp.bfloat16)
@@ -294,7 +377,6 @@
         per = max(1, halo // n_group)
         gram_rows = width // n_group
         vmem = pl.BlockSpec(memory_space=pltpu.VMEM)
-        smem = pl.BlockSpec(memory_space=pltpu.SMEM)
         dma = pltpu.SemaphoreType.DMA
         return pl.pallas_call(
             functools.partial(kernel, n_dom, n_group, halo, rows_dev * n_dom * n_group),
@@ -302,10 +384,18 @@
                 jax.ShapeDtypeStruct((width, rows_dev), jnp.bfloat16),
                 jax.ShapeDtypeStruct((width, width), jnp.float32),
             ),
-            in_specs=[vmem, pl.BlockSpec(memory_space=pl.ANY), smem, smem, smem, smem],
+            in_specs=[pl.BlockSpec(memory_space=pltpu.HBM)] * 6,
             out_specs=(vmem, vmem),
             scratch_shapes=(
-                [pltpu.VMEM((in_part, width, block), jnp.bfloat16)] * n_apply
+                [
+                    pltpu.VMEM(start.shape, start.dtype),
+                    pltpu.SMEM(row_ptr.shape, jnp.int32),
+                    pltpu.SMEM(col_part.shape, jnp.int32),
+                    pltpu.SMEM(col_local.shape, jnp.int32),
+                    pltpu.SMEM(halo_list.shape, jnp.int32),
+                    dma((5,)),
+                ]
+                + [pltpu.VMEM((in_part, width, block), jnp.bfloat16)] * n_apply
                 + [pltpu.VMEM((n_dom * halo, width, block), jnp.bfloat16)] * n_apply
                 + [pltpu.VMEM((n_dom, per, width, block), jnp.bfloat16)] * n_apply
                 + [
@@ -319,7 +409,7 @@
                 + [pltpu.VMEM((n_dom, gram_rows, block), jnp.float32)] * n_apply
                 + [pltpu.VMEM((n_group, gram_rows, block), jnp.float32)] * n_apply
                 + [dma((slots // CHUNK,))]
-                + [dma((n_apply, n_group))] * 2
+                + [dma((n_apply, max(6, n_group)))] * 2
                 + [dma((n_apply, n_dom))] * 2
                 + [dma((n_apply, n_dom, n_group))] * 2
                 + [dma((n_apply, n_group))] * 2

time: 94.7 us -> 86.5 us (0.913)
  Pallas kernels: 87.4 us -> 79.2 us
    pallas_call x1, Pallas kernels: 87.4 us -> 79.2 us  [step(): pl.pallas_call(functools.partial(kernel, n_dom, n_group, halo, rows_dev *...]
where the time goes in v2:
time: 86.5 us; the launch traced here: 86.3 us
  Pallas kernels  79.2 us (92%)
  local copies, waits for them, and re-layouts  6.49 us (8%)
    pallas_call x1, Pallas kernels, step(): pl.pallas_call(functools.partial(kernel, n_dom, n_group, halo, rows_dev *...  79.2 us
    unnamed x13, local copies, waits for them, and re-layouts  6.49 us

profile of v2, /device:TPU:0, one launch (start us, length us, event | category | flops | bytes accessed | tf_op | source)
XLA Modules:
  0.0 86.3 jit_solution(4710273639926781774)
XLA Ops:
  0.6 0.8 copy.8.refs_5_
  1.4 0.0 copy-start
  1.4 1.6 %copy-done = s32[1,32,128,128]{3,2,1,0:T(8,128)S(1)} copy-done((s32[1,32,128,128]{3,2,1,0:T(8,128)S(1)}, s32[1,32,128,128]{3,2,1,0:T(8,128)}, u32[]{:S(2)}) %copy-start) | copy-done | bytes 2097176
  3.0 0.0 copy-start.1
  3.0 0.9 %copy-done.1 = bf16[64,1024]{1,0:T(8,128)(2,1)S(1)} copy-done((bf16[64,1024]{1,0:T(8,128)(2,1)S(1)}, bf16[64,1024]{1,0:T(8,128)(2,1)}, u32[]{:S(2)}) %copy-start.1) | copy-done | bytes 131096
  3.9 0.0 copy-start.2
  3.9 0.7 copy-done.2
  4.5 0.0 copy-start.3
  4.5 0.7 copy-done.3
  5.2 0.0 copy-start.4
  5.2 0.7 copy-done.4
  5.8 79.2 %shard_map.77 = (bf16[64,1024]{1,0:T(8,128)(2,1)S(1)}, f32[64,64]{1,0:T(8,128)S(1)}) custom-call(bf16[64,1024]{1,0:T(8,128)(2,1)S(1)} %copy-done.1, s32[1,32,128,128]{3,2,1,0:T(8,128)S(1)} %copy-done, s32[1,9]{1,0:T(1,128)S(1)} %copy-done.2, s32[1,32]{1,0:T(1,128)S(1)} %copy-done.3, s32[1,32]{1,0:T(1,128)S(1)} %copy-done.4, s32[1,8,4]{2,1,0:T(8,128)S(1)} %copy.8.refs_5_), custom_call_target="tpu_custom_call" | custom-call | tf_op jit(solution)/shard_map/pallas_call | solution.py:381
  85.0 0.7 copy.11
  85.7 0.6 copy.12
Async XLA Ops:
  1.4 1.6 %copy-start = (s32[1,32,128,128]{3,2,1,0:T(8,128)S(1)}, s32[1,32,128,128]{3,2,1,0:T(8,128)}, u32[]{:S(2)}) copy-start(s32[1,32,128,128]{3,2,1,0:T(8,128)} %refs_1_.1) | copy-start | bytes 6291460
  3.0 0.9 %copy-start.1 = (bf16[64,1024]{1,0:T(8,128)(2,1)S(1)}, bf16[64,1024]{1,0:T(8,128)(2,1)}, u32[]{:S(2)}) copy-start(bf16[64,1024]{1,0:T(8,128)(2,1)} %refs_0_.1) | copy-start | bytes 393220
  3.9 0.7 copy-start.2
  4.5 0.7 copy-start.3
  5.2 0.7 copy-start.4

commit v3 on v2

--- a/solution.py
+++ b/solution.py
@@ -175,14 +175,7 @@
         return remote(halos[a].at[place], halos[a].at[place], s3.at[a, o, index], r3.at[a, o, index], (own, to))
 
     def third_copies(a, o):
-        if relayed:
-            return [third_copy(a, o, me, 0, across), third_copy(a, o, me, 1, along)]
         return [third_copy(a, o, me, j, beside(j)) for j in range(1, n_group)]
-
-    def third_relay(a, o):
-        if doms.index(o) % 2:
-            return third_copy(a, o, along, 2, across)
-        return third_copy(a, o, across, 2, along)
 
     def exchange_second(a):
         rest = first_copies(a)[2:] + relay_copies(a) if relayed else first_copies(a)
@@ -208,14 +201,6 @@
         as_sender(me, body)
 
     def exchange_end(a):
-        if relayed:
-            for o in doms:
-                for copy in third_copies(a, o):
-                    copy.wait_recv()
-                third_relay(a, o).start()
-            for o in doms:
-                third_relay(a, o).wait_recv()
-            return
         for o in doms:
             for j, copy in zip(range(1, n_group), third_copies(a, o)):
                 as_sender(beside(n_group - j), copy.wait_recv)
@@ -229,8 +214,6 @@
                 copy.wait_send()
                 for spread in third_copies(a, o):
                     spread.wait_send()
-                if relayed:
-                    third_relay(a, o).wait_send()
 
         as_sender(me, body)
 
@@ -417,7 +400,7 @@
                 + [dma((n_apply, n_group))] * 2
             ),
             compiler_params=pltpu.CompilerParams(
-                collective_id=0, has_side_effects=True, vmem_limit_bytes=48 * 1024 * 1024
+                collective_id=0, has_side_effects=True, vmem_limit_bytes=67043328
             ),
         )(start, tiles, row_ptr, col_part, col_local, halo_list)
 

time: 86.5 us -> 82 us (0.948)
  Pallas kernels: 79.2 us -> 76.8 us
  local copies, waits for them, and re-layouts: 6.49 us -> 4.29 us
    pallas_call x1, Pallas kernels: 79.2 us -> 76.8 us  [step(): pl.pallas_call(functools.partial(kernel, n_dom, n_group, halo, rows_dev *...]
    unnamed x13 -> x3, local copies, waits for them, and re-layouts: 6.49 us -> 4.29 us
where the time goes in v3:
time: 82 us; the launch traced here: 81.7 us
  Pallas kernels  76.8 us (94%)
  local copies, waits for them, and re-layouts  4.29 us (5%)
    pallas_call x1, Pallas kernels, step(): pl.pallas_call(functools.partial(kernel, n_dom, n_group, halo, rows_dev *...  76.8 us
    unnamed x3, local copies, waits for them, and re-layouts  4.29 us

profile of v3, /device:TPU:0, one launch (start us, length us, event | category | flops | bytes accessed | tf_op | source)
XLA Modules:
  0.0 81.7 jit_solution(3022437695471302204)
XLA Ops:
  0.6 1.3 %copy.8.refs_5_ = s32[1,8,4]{2,1,0:T(8,128)} copy(s32[1,8,4]{1,2,0:T(4,128)} %param.11) | data formatting | bytes 256 | tf_op args[5]
  2.0 76.8 %shard_map.77 = (bf16[64,1024]{1,0:T(8,128)(2,1)}, f32[64,64]{1,0:T(8,128)}) custom-call(bf16[64,1024]{1,0:T(8,128)(2,1)} %refs_0_.1, s32[1,32,128,128]{3,2,1,0:T(8,128)} %refs_1_.1, s32[1,9]{1,0:T(1,128)} %refs_2_.1, s32[1,32]{1,0:T(1,128)} %refs_3_.1, s32[1,32]{1,0:T(1,128)} %refs_4_.1, s32[1,8,4]{2,1,0:T(8,128)} %copy.8.refs_5_), custom_call_target="tpu_custom_call" | custom-call | tf_op jit(solution)/shard_map/pallas_call | solution.py:364
  78.8 1.6 %copy.11 = bf16[64,1024]{1,0:T(8,128)(2,1)} copy(bf16[64,1024]{1,0:T(8,128)(2,1)} %get-tuple-element.4) | data formatting | bytes 262144
  80.4 1.4 %copy.12 = f32[64,64]{1,0:T(8,128)} copy(f32[64,64]{1,0:T(8,128)} %get-tuple-element.5) | data formatting | bytes 32768
